TPU v7x, 32 devices: a whole 2x2x4 slice. The times are simulated.
32 devices in a mesh: pair: 2 (over core), lat: 4 (over y, x), tok: 4 (over z).
Axes of the slice: x: 2, y: 2, z: 4, core: 2. Of those that a mesh axis runs over, the one named last changes fastest.
Arguments:
- residual: bfloat16 [2, 512, 4096], P('pair', 'tok', 'lat'), may hold values from -6 to 6
- matches: int32 [2, 512], P('pair', 'tok'), may hold values from 0 to 511, as said below
- kl_grad: bfloat16 [512, 4096], P('tok', 'lat'), may hold values from -6 to 6
- active_blocks: int32 [64, 2], replicated, may hold values from 0 to 31, all different within a row; in each aligned block of 16 rows (0 to 15, 16 to 31, ...) at most 2 rows name the same one
- encoder: bfloat16 [4096, 4096], P(None, ('pair', 'lat', 'tok')), may hold values from -0.09375 to 0.09375
- encoder_offset_bias: float32 [4096], P(('pair', 'lat', 'tok')), may hold values from -3 to 3
- decoder: bfloat16 [4096, 4096], P(('pair', 'lat', 'tok')), may hold values from -0.5 to 0.5
- dec_bias: float32 [4096], P('lat'), may hold values from -3 to 3
Outputs:
- reconstruction: bfloat16 [512, 4096], P('tok', 'lat')
- scores: float32 [4096], P(('pair', 'lat', 'tok'))
Inputs may be any that keep to these rules, and one draw needn't show every extreme that they name: For each model m and matched token k: k - 128 < matches[m, k] <= k (at least 0); where k is a positive multiple of 128, matches[m, k] = k - 127. `active_blocks`: each row lists 2 different latent blocks. Among the 16 rows of one tok index (aligned blocks of rows) no latent block is listed more than 2 times, and some latent block is listed exactly 2 times.
All inputs are finite; a program needn't handle non-finite values.
Results may differ from a plain program's by a relative error of at most 0.0085.
Values may be sent and summed in bfloat16 or wider, within the bound.
A program may use at most 64 MiB of HBM per device.

v0:
```python
import math
import jax
import jax.numpy as jnp
from jax import lax
from jax.sharding import PartitionSpec as P

TBLK = 8
MOST = 2


def passed_along(x, axis, by):
    devices = lax.axis_size(axis)
    pairs = [(i, i + by) for i in range(devices) if 0 <= i + by < devices]
    return lax.ppermute(x, axis, pairs)


def from_partner(x, axis, bit):
    return lax.ppermute(x, axis, [(i, i ^ 1 << bit) for i in range(lax.axis_size(axis))])


def slot_table(my_lists, targets, slot_ids):
    listed = jnp.any(my_lists[:, :, None] == targets[None, None, :], axis=1).astype(jnp.int32)
    ranking = jnp.cumsum(listed, axis=0) - listed
    return (listed.T[:, None, :] * (ranking.T[:, None, :] == slot_ids[None, :, None])).astype(
        jnp.bfloat16
    )


def shards(
    residual, matches, kl_grad, active_blocks, encoder, encoder_offset_bias, decoder, dec_bias
):
    tok_dev = residual.shape[1]
    tok_count = lax.axis_size("tok")
    lat_count = lax.axis_size("lat")
    tok_here = lax.axis_index("tok")
    own_rows = residual[0]
    earlier = passed_along(own_rows, "tok", 1)
    window = jnp.concatenate([earlier, own_rows], axis=0)
    first_row = (tok_here - 1) * tok_dev
    local_index = matches[0] - first_row
    matched = jnp.take(window, local_index, axis=0)
    partner = from_partner(matched, "pair", 0)
    is_chat = lax.axis_index("pair") == 1
    chat_rows = jnp.where(is_chat, matched, partner)
    base_rows = jnp.where(is_chat, partner, matched)
    delta_rows = (chat_rows.astype(jnp.float32) - base_rows.astype(jnp.float32)).astype(
        jnp.bfloat16
    )
    tb_dev = tok_dev // TBLK
    pair_base = lax.axis_index("pair") * lat_count
    row_base = (pair_base + lax.axis_index("lat")) * tok_count
    my_block = row_base + tok_here
    my_lists = lax.dynamic_slice_in_dim(active_blocks, tok_here * tb_dev, tb_dev, 0)
    slot_ids = jnp.arange(MOST, dtype=jnp.int32)
    targets = row_base + jnp.arange(tok_count, dtype=jnp.int32)
    chooser = slot_table(my_lists, targets, slot_ids)
    mine_listed = jnp.any(active_blocks == my_block, axis=1).astype(jnp.int32)
    counts = jnp.sum(mine_listed.reshape(tok_count, tb_dev), axis=1)
    padded_output = (slot_ids[None, :] < counts[:, None]).astype(jnp.float32)[:, :, None, None]

    def select_slots(blocks):
        return jnp.einsum(
            "ksb,btd->kstd", chooser, blocks, preferred_element_type=jnp.float32
        ).astype(jnp.bfloat16)

    full_delta, full_grad = (
        lax.all_gather(delta_rows, "lat", axis=1, tiled=True),
        lax.all_gather(kl_grad, "lat", axis=1, tiled=True),
    )
    full_width = full_delta.shape[1]
    sent_delta = select_slots(full_delta.reshape(tb_dev, TBLK, full_width))
    sent_grad = select_slots(full_grad.reshape(tb_dev, TBLK, full_width))
    got_delta, got_grad = (
        lax.all_to_all(sent_delta, "tok", split_axis=0, concat_axis=0, tiled=True),
        lax.all_to_all(sent_grad, "tok", split_axis=0, concat_axis=0, tiled=True),
    )
    preactivation = jnp.einsum(
        "kstd,dc->kstc", got_delta, encoder, preferred_element_type=jnp.float32
    )
    gradient_inner_product = jnp.einsum(
        "kstd,cd->kstc", got_grad, decoder, preferred_element_type=jnp.float32
    )
    activation_value = jnp.maximum(preactivation + encoder_offset_bias, 0.0) * padded_output
    every_token_rows = tok_dev * tok_count
    scores = jnp.sum(activation_value * gradient_inner_product, axis=(0, 1, 2)) / math.sqrt(
        every_token_rows / 8
    )
    activation_half_precision = activation_value.astype(jnp.bfloat16)
    pieces_out = jnp.einsum(
        "fazg,gh->fazh", activation_half_precision, decoder, preferred_element_type=jnp.float32
    ).astype(jnp.bfloat16)
    returned = lax.all_to_all(pieces_out, "tok", split_axis=0, concat_axis=0, tiled=True)
    source_sums = jnp.einsum(
        "ksb,kstd->btd", chooser, returned, preferred_element_type=jnp.float32
    ).reshape(tok_dev, -1)
    shared = lax.psum_scatter(
        source_sums.astype(jnp.bfloat16), "lat", scatter_dimension=1, tiled=True
    )
    summed = lax.psum(shared, "pair").astype(jnp.float32)
    return ((summed + dec_bias).astype(jnp.bfloat16), scores)


def solution(mesh):
    placed = (
        P("pair", "tok", "lat"),
        P("pair", "tok"),
        P("tok", "lat"),
        P(),
        P(None, ("pair", "lat", "tok")),
        P(("pair", "lat", "tok")),
        P(("pair", "lat", "tok"), None),
        P("lat"),
    )
    return jax.shard_map(
        shards,
        mesh=mesh,
        in_specs=placed,
        out_specs=(P("tok", "lat"), P(("pair", "lat", "tok"))),
        check_vma=False,
    )
```

profile of v0, /device:TPU:0, one launch (start us, length us, event | category | flops | bytes accessed | tf_op | source)
XLA Modules:
  0.0 148.8 jit_solution(7111867988648437557)
XLA Ops:
  7.2 0.0 copy-start
  7.2 0.0 all-gather.3.cloned.1.call-start
  7.2 5.1 %collective-permute-start = (bf16[128,1024]{1,0:T(8,128)(2,1)}, bf16[128,1024]{1,0:T(8,128)(2,1)S(1)}, u32[]{:S(2)}, u32[]{:S(2)}) collective-permute-start(bf16[128,1024]{1,0:T(8,128)(2,1)} %bitcast.56), channel_id=1, source_target_pairs={{0,1},{1,2},{2,3},{4,5},{5,6},{6,7},{8,9},{9,10},{10,11},{12,13},{... | collective-permute-start | bytes 786440 | tf_op jit(solution)/shard_map/ppermute | solution.py:14
  12.3 0.7 fusion.20
  13.0 0.7 compare_and_fusion
  13.7 4.5 %collective-permute-done = bf16[128,1024]{1,0:T(8,128)(2,1)S(1)} collective-permute-done((bf16[128,1024]{1,0:T(8,128)(2,1)}, bf16[128,1024]{1,0:T(8,128)(2,1)S(1)}, u32[]{:S(2)}, u32[]{:S(2)}) %collective-permute-start) | collective-permute-done | bytes 262176 | tf_op jit(solution)/shard_map/ppermute | solution.py:14
  18.2 1.0 pad_maximum_fusion
  19.2 0.9 gather_fusion
  20.0 0.1 broadcast_select_fusion
  20.1 0.1 collective-permute-start.1
  20.2 1.5 %collective-permute-done.1 = bf16[128,1024]{1,0:T(8,128)(2,1)S(1)} collective-permute-done((bf16[128,1024]{1,0:T(8,128)(2,1)S(1)}, bf16[128,1024]{1,0:T(8,128)(2,1)S(1)}, u32[]{:S(2)}, u32[]{:S(2)}) %collective-permute-start.1) | collective-permute-done | bytes 262176 | tf_op jit(solution)/shard_map/ppermute | solution.py:18
  21.7 0.9 subtract_convert_fusion
  22.6 0.0 all-gather.3.cloned.1.call-update
  22.7 0.1 constant_dynamic-slice_fusion
  22.8 0.1 compare_reduce_fusion
  22.9 0.1 copy.48
  23.0 0.1 copy.49
  23.1 0.1 copy.50
  23.2 28.2 %all-gather.3.cloned.1.call-done = bf16[128,4096]{1,0:T(8,128)(2,1)} async-done(((bf16[128,1024]{1,0:T(8,128)(2,1)}), bf16[128,4096]{1,0:T(8,128)(2,1)}) %all-gather.3.cloned.1.call-update) | async-done | bytes 1048592 | tf_op jit(solution)/shard_map/all_gather | solution.py:67
  51.4 2.5 %convolution_convert_fusion.1 = bf16[4,2,8,4096]{3,0,2,1:T(4,128)(2,1)S(1)} fusion(bf16[16,8,4096]{2,1,0:T(8,128)(2,1)} %bitcast.54, s32[4,16]{1,0:T(4,128)S(1)} %copy.50, s32[4,16]{1,0:T(4,128)S(1)} %copy.49), kind=kOutput, calls=%fused_computation.4 | convolution fusion | flops 8651136 | bytes 1573376 | tf_op jit(solution)/shard_map/ksb,btd->kstd/dot_general | solution.py:62
  53.8 0.0 copy-start.1
  53.9 0.0 copy-start.4
  53.9 1.1 copy.52
  55.0 4.6 %all-to-all-start = ((bf16[4,2,8,4096]{3,2,1,0:T(8,128)(2,1)}), bf16[4,2,8,4096]{3,2,1,0:T(8,128)(2,1)S(1)}, u32[]{:S(2)}, u32[]{:S(2)}) async-start(bf16[4,2,8,4096]{3,2,1,0:T(8,128)(2,1)} %copy.52), calls=%async_computation | async-start | bytes 1048576 | tf_op jit(solution)/shard_map/all_to_all | solution.py:74
  59.6 0.7 all-gather.5.cloned.1.call-update
  60.3 0.0 reduce-scatter.2.cloned.1.call-start
  60.4 0.1 reshape.78
  60.5 0.1 reduce_sum.18
  60.6 0.1 fusion.19
  60.7 13.2 %all-to-all-done = bf16[4,2,8,4096]{3,2,1,0:T(8,128)(2,1)S(1)} async-done(((bf16[4,2,8,4096]{3,2,1,0:T(8,128)(2,1)}), bf16[4,2,8,4096]{3,2,1,0:T(8,128)(2,1)S(1)}, u32[]{:S(2)}, u32[]{:S(2)}) %all-to-all-start) | async-done | bytes 524320 | tf_op jit(solution)/shard_map/all_to_all | solution.py:74
  73.9 0.3 fusion.25
  74.2 0.3 convolution_convert_fusion.2
  74.5 0.5 copy.54
  75.1 16.4 %all_to_all.15 = bf16[4,2,8,4096]{3,1,2,0:T(2,128)(2,1)S(1)} all-to-all(bf16[4,2,8,4096]{3,1,2,0:T(2,128)(2,1)S(1)} %copy.54), channel_id=1, replica_groups=mesh['pair'=2,'lat'=4,'tok'=4] {'tok'}, dimensions={0} | all-to-all | bytes 1048576 | tf_op jit(solution)/shard_map/all_to_all | solution.py:92
  91.5 0.7 fusion
  92.2 1.6 %copy.76 = bf16[16,8,4096]{2,1,0:T(8,128)(2,1)} copy(bf16[16,8,4096]{2,0,1:T(8,128)(2,1)S(1)} %fusion) | data formatting | bytes 2097152 | tf_op jit(solution)/shard_map/convert_element_type | solution.py:97
  93.8 0.0 reduce-scatter.2.cloned.1.call-update
  93.9 0.0 all-gather.5.cloned.1.call-done
  93.9 2.5 %convolution_convert_fusion = bf16[4,2,8,4096]{3,0,2,1:T(4,128)(2,1)S(1)} fusion(bf16[16,8,4096]{2,1,0:T(8,128)(2,1)} %bitcast.55, s32[4,16]{1,0:T(4,128)S(1)} %copy.50, s32[4,16]{1,0:T(4,128)S(1)} %copy.49), kind=kOutput, calls=%fused_computation.3 | convolution fusion | flops 8651136 | bytes 1573376 | tf_op jit(solution)/shard_map/ksb,btd->kstd/dot_general | solution.py:62
  96.3 1.1 copy.58
  97.4 3.5 %all-to-all-start.2 = ((bf16[4,2,8,4096]{3,2,1,0:T(8,128)(2,1)}), bf16[4,2,8,4096]{3,2,1,0:T(8,128)(2,1)S(1)}, u32[]{:S(2)}, u32[]{:S(2)}) async-start(bf16[4,2,8,4096]{3,2,1,0:T(8,128)(2,1)} %copy.58), calls=%async_computation.3 | async-start | bytes 1048576 | tf_op jit(solution)/shard_map/all_to_all | solution.py:75
  100.9 0.0 all-reduce.2.cloned.1.call-start
  101.0 19.1 %reduce-scatter.2.cloned.1.call-done = bf16[128,1024]{1,0:T(8,128)(2,1)} async-done(((bf16[128,4096]{1,0:T(8,128)(2,1)}), bf16[128,1024]{1,0:T(8,128)(2,1)}) %reduce-scatter.2.cloned.1.call-update) | async-done | bytes 262160 | tf_op jit(solution)/shard_map/reduce_scatter | solution.py:96
  120.1 0.0 all-reduce.2.cloned.1.call-update
  120.1 0.5 fusion.3
  120.6 0.5 broadcast_multiply_fusion
  121.1 19.4 %all-reduce.2.cloned.1.call-done = bf16[128,1024]{1,0:T(8,128)(2,1)} async-done(((bf16[128,1024]{1,0:T(8,128)(2,1)}), bf16[128,1024]{1,0:T(8,128)(2,1)}) %all-reduce.2.cloned.1.call-update) | async-done | bytes 262160 | tf_op jit(solution)/shard_map/psum | solution.py:99
  140.5 1.7 %add_convert_fusion = bf16[128,1024]{1,0:T(8,128)(2,1)} fusion(bf16[128,1024]{1,0:T(8,128)(2,1)} %all-reduce.2.cloned.1.call-done, f32[1024]{0:T(1024)S(1)} %copy-done.2), kind=kLoop, calls=%fused_computation.21 | loop fusion | flops 393216 | bytes 528384 | tf_op jit(solution)/shard_map/convert_element_type | solution.py:100
  (16 shorter events, 0.1 us)
Async XLA Ops:
  7.2 67.0 %copy-start = (bf16[128,4096]{1,0:T(8,128)(2,1)S(1)}, bf16[128,4096]{1,0:T(8,128)(2,1)}, u32[]{:S(2)}) copy-start(bf16[128,4096]{1,0:T(8,128)(2,1)} %param.14) | copy-start | bytes 3145732
  7.2 44.2 %all-gather.3.cloned.1.call-start = ((), (), s32[]{:S(2)}) async-start(), calls=%async_computation.4 | async-start | bytes 1310720 | tf_op jit(solution)/shard_map/all_gather | solution.py:67
  7.2 11.0 %collective-permute-start = (bf16[128,1024]{1,0:T(8,128)(2,1)}, bf16[128,1024]{1,0:T(8,128)(2,1)S(1)}, u32[]{:S(2)}, u32[]{:S(2)}) collective-permute-start(bf16[128,1024]{1,0:T(8,128)(2,1)} %bitcast.56), channel_id=1, source_target_pairs={{0,1},{1,2},{2,3},{4,5},{5,6},{6,7},{8,9},{9,10},{10,11},{12,13},{... | collective-permute-start | bytes 786440 | tf_op jit(solution)/shard_map/ppermute | solution.py:14
  20.0 2.7 %copy-start.3 = (s32[64,2]{0,1:T(2,128)S(1)}, s32[64,2]{0,1:T(2,128)}, u32[]{:S(2)}) copy-start(s32[64,2]{0,1:T(2,128)} %param.11) | copy-start | bytes 1540
  20.1 1.6 %collective-permute-start.1 = (bf16[128,1024]{1,0:T(8,128)(2,1)S(1)}, bf16[128,1024]{1,0:T(8,128)(2,1)S(1)}, u32[]{:S(2)}, u32[]{:S(2)}) collective-permute-start(bf16[128,1024]{1,0:T(8,128)(2,1)S(1)} %broadcast_select_fusion), channel_id=1, source_target_pairs={{0,16},{16,0},{1,17},{17,1},{2,18},{18,2},{3,19},{19,3},{4,20},{20... | collective-permute-start | bytes 786440 | tf_op jit(solution)/shard_map/ppermute | solution.py:18
  53.8 20.1 %copy-start.1 = (bf16[4096,128]{1,0:T(8,128)(2,1)S(1)}, bf16[4096,128]{1,0:T(8,128)(2,1)}, u32[]{:S(2)}) copy-start(bf16[4096,128]{1,0:T(8,128)(2,1)} %param.12) | copy-start | bytes 3145732
  53.9 20.0 %copy-start.4 = (f32[128]{0:T(128)S(1)}, f32[128]{0:T(128)}, u32[]{:S(2)}) copy-start(f32[128]{0:T(128)} %param.13) | copy-start | bytes 1540
  55.0 18.9 %all-to-all-start = ((bf16[4,2,8,4096]{3,2,1,0:T(8,128)(2,1)}), bf16[4,2,8,4096]{3,2,1,0:T(8,128)(2,1)S(1)}, u32[]{:S(2)}, u32[]{:S(2)}) async-start(bf16[4,2,8,4096]{3,2,1,0:T(8,128)(2,1)} %copy.52), calls=%async_computation | async-start | bytes 1048576 | tf_op jit(solution)/shard_map/all_to_all | solution.py:74
  59.6 34.3 %all-gather.5.cloned.1.call-start = ((), (), s32[]{:S(2)}) async-start(), calls=%async_computation.7 | async-start | bytes 1310720 | tf_op jit(solution)/shard_map/all_gather | solution.py:68
  60.3 59.8 %reduce-scatter.2.cloned.1.call-start = ((), (), s32[]{:S(2)}) async-start(), calls=%async_computation.5 | async-start | bytes 1310720 | tf_op jit(solution)/shard_map/reduce_scatter | solution.py:96
  97.4 22.7 %all-to-all-start.2 = ((bf16[4,2,8,4096]{3,2,1,0:T(8,128)(2,1)}), bf16[4,2,8,4096]{3,2,1,0:T(8,128)(2,1)S(1)}, u32[]{:S(2)}, u32[]{:S(2)}) async-start(bf16[4,2,8,4096]{3,2,1,0:T(8,128)(2,1)} %copy.58), calls=%async_computation.3 | async-start | bytes 1048576 | tf_op jit(solution)/shard_map/all_to_all | solution.py:75
  100.9 39.6 %copy-start.2 = (f32[1024]{0:T(1024)S(1)}, f32[1024]{0:T(1024)}, u32[]{:S(2)}) copy-start(f32[1024]{0:T(1024)} %param.15) | copy-start | bytes 12292
  100.9 39.6 %all-reduce.2.cloned.1.call-start = ((), (), s32[]{:S(2)}) async-start(), calls=%async_computation.6 | async-start | bytes 524288 | tf_op jit(solution)/shard_map/psum | solution.py:99
Sparse Core Ops, SparseCore 0:
  22.8 28.5 all-gather.2
  62.2 26.9 all-gather.4
  94.0 26.0 reduce-scatter.1
  122.3 18.2 all-reduce.1
where the time goes:
time: 149 us
  waiting for transfers between devices  86.7 us (58%)
  blocking collectives  16.4 us (11%)
  between operations  13.9 us (9%)
  starting transfers between devices  13.4 us (9%)
  matrix products  6.75 us (5%)
  other arithmetic  5.9 us (4%)
  local copies, waits for them, and re-layouts  5.64 us (4%)
    all_gather x1, waiting for transfers between devices, shards(): lax.all_gather(delta_rows, 'lat', axis=1, tiled=True)  28.2 us
    psum x1, waiting for transfers between devices, shards(): summed = lax.psum(shared, 'pair').astype(jnp.float32)  19.4 us
    reduce_scatter x1, waiting for transfers between devices, shards(): lax.psum_scatter(source_sums.astype(jnp.bfloat16), 'lat', scatter_dimensi...  19.1 us
    all_to_all x1, blocking collectives, shards(): lax.all_to_all(pieces_out, 'tok', split_axis=0, concat_axis=0, tiled=True)  16.4 us
    all_to_all x1, waiting for transfers between devices, shards(): lax.all_to_all(sent_delta, 'tok', split_axis=0, concat_axis=0, tiled=True)  13.2 us
    ppermute x1, starting transfers between devices, passed_along(): return lax.ppermute(x, axis, pairs)  5.11 us
    dot_general x2, matrix products, select_slots(): jnp.einsum('ksb,btd->kstd', chooser, blocks, preferred_element_type=jnp.f...  4.93 us
    all_to_all x1, starting transfers between devices, shards(): lax.all_to_all(sent_delta, 'tok', split_axis=0, concat_axis=0, tiled=True)  4.6 us
  transfers between devices with their start and end apart: 8, of which 6 were waited for; matrix products, arithmetic and copies ran while one was open for 7% of the time, Pallas kernels for 0%

commit v1 on v0

--- a/solution.py
+++ b/solution.py
@@ -6,6 +6,22 @@
 
 TBLK = 8
 MOST = 2
+
+
+def collect(x, axis, dim):
+    ways, here, step = (lax.axis_size(axis), lax.axis_index(axis), x.shape[dim])
+    lengths = [n * ways if d == dim else n for d, n in enumerate(x.shape)]
+    full = lax.dynamic_update_slice_in_dim(jnp.zeros(lengths, x.dtype), x, here * step, axis=dim)
+    going_up = going_down = x
+    for far in range(1, ways // 2 + 1):
+        going_up = lax.ppermute(going_up, axis, [(d, (d + 1) % ways) for d in range(ways)])
+        full = lax.dynamic_update_slice_in_dim(full, going_up, (here - far) % ways * step, axis=dim)
+        if 2 * far < ways:
+            going_down = lax.ppermute(going_down, axis, [(d, (d - 1) % ways) for d in range(ways)])
+            full = lax.dynamic_update_slice_in_dim(
+                full, going_down, (here + far) % ways * step, axis=dim
+            )
+    return full
 
 
 def passed_along(x, axis, by):
@@ -64,7 +80,7 @@
         ).astype(jnp.bfloat16)
 
     full_delta, full_grad = (
-        lax.all_gather(delta_rows, "lat", axis=1, tiled=True),
+        collect(delta_rows, "lat", 1),
         lax.all_gather(kl_grad, "lat", axis=1, tiled=True),
     )
     full_width = full_delta.shape[1]

time: 149 us -> 140 us (0.940)
  waiting for transfers between devices: 86.7 us -> 75.1 us
  starting transfers between devices: 13.4 us -> 18 us
    all_gather x1 -> x0, waiting for transfers between devices: 28.2 us -> none  [shards(): lax.all_gather(delta_rows, 'lat', axis=1, tiled=True)]
    ppermute x0 -> x3, waiting for transfers between devices: none -> 16.5 us  [the longest x2 11.6 us: collect(): lax.ppermute(going_up, axis, [(d, (d + 1) % ways) for d in range(ways)])]
    ppermute x0 -> x3, starting transfers between devices: none -> 3.61 us  [the longest x2 2.14 us: collect(): lax.ppermute(going_up, axis, [(d, (d + 1) % ways) for d in range(ways)])]
  transfers between devices with their start and end apart: 8 -> 10, of which waited for: 6 -> 8; matrix products, arithmetic and copies ran while one was open for 7% -> 7% of each run, Pallas kernels for 0% -> 0%
where the time goes in v1:
time: 140 us
  waiting for transfers between devices  75.1 us (54%)
  starting transfers between devices  18 us (13%)
  blocking collectives  16.5 us (12%)
  between operations  13.9 us (10%)
  local copies, waits for them, and re-layouts  5.8 us (4%)
  matrix products  5.52 us (4%)
  other arithmetic  5.2 us (4%)
    reduce_scatter x1, waiting for transfers between devices, shards(): lax.psum_scatter(source_sums.astype(jnp.bfloat16), 'lat', scatter_dimensi...  19.6 us
    psum x1, waiting for transfers between devices, shards(): summed = lax.psum(shared, 'pair').astype(jnp.float32)  19.5 us
    all_to_all x1, blocking collectives, shards(): lax.all_to_all(pieces_out, 'tok', split_axis=0, concat_axis=0, tiled=True)  16.5 us
    all_to_all x1, waiting for transfers between devices, shards(): lax.all_to_all(sent_delta, 'tok', split_axis=0, concat_axis=0, tiled=True)  12.9 us
    ppermute x2, waiting for transfers between devices, collect(): lax.ppermute(going_up, axis, [(d, (d + 1) % ways) for d in range(ways)])  11.6 us
    all_to_all x1, starting transfers between devices, shards(): lax.all_to_all(sent_delta, 'tok', split_axis=0, concat_axis=0, tiled=True)  5.67 us
    ppermute x1, starting transfers between devices, passed_along(): return lax.ppermute(x, axis, pairs)  5.11 us
    ppermute x1, waiting for transfers between devices, collect(): lax.ppermute(going_down, axis, [(d, (d - 1) % ways) for d in range(ways)])  4.88 us
  transfers between devices with their start and end apart: 10, of which 8 were waited for; matrix products, arithmetic and copies ran while one was open for 7% of the time, Pallas kernels for 0%

profile of v1, /device:TPU:0, one launch (start us, length us, event | category | flops | bytes accessed | tf_op | source)
XLA Modules:
  0.0 140.0 jit_solution(4096357669691139438)
XLA Ops:
  7.2 5.1 %collective-permute-start = (bf16[128,1024]{1,0:T(8,128)(2,1)}, bf16[128,1024]{1,0:T(8,128)(2,1)S(1)}, u32[]{:S(2)}, u32[]{:S(2)}) collective-permute-start(bf16[128,1024]{1,0:T(8,128)(2,1)} %bitcast.56), channel_id=1, source_target_pairs={{0,1},{1,2},{2,3},{4,5},{5,6},{6,7},{8,9},{9,10},{10,11},{12,13},{... | collective-permute-start | bytes 786440 | tf_op jit(solution)/shard_map/ppermute | solution.py:30
  12.3 0.7 fusion.21
  13.0 0.7 compare_and_fusion
  13.6 4.5 %collective-permute-done = bf16[128,1024]{1,0:T(8,128)(2,1)S(1)} collective-permute-done((bf16[128,1024]{1,0:T(8,128)(2,1)}, bf16[128,1024]{1,0:T(8,128)(2,1)S(1)}, u32[]{:S(2)}, u32[]{:S(2)}) %collective-permute-start) | collective-permute-done | bytes 262176 | tf_op jit(solution)/shard_map/ppermute | solution.py:30
  18.1 1.0 pad_maximum_fusion
  19.1 0.9 gather_fusion
  20.0 0.1 broadcast_select_fusion
  20.1 0.1 collective-permute-start.1
  20.2 0.1 constant_dynamic-slice_fusion
  20.3 1.4 %collective-permute-done.1 = bf16[128,1024]{1,0:T(8,128)(2,1)S(1)} collective-permute-done((bf16[128,1024]{1,0:T(8,128)(2,1)S(1)}, bf16[128,1024]{1,0:T(8,128)(2,1)S(1)}, u32[]{:S(2)}, u32[]{:S(2)}) %collective-permute-start.1) | collective-permute-done | bytes 262176 | tf_op jit(solution)/shard_map/ppermute | solution.py:34
  21.7 0.1 broadcast_in_dim.12
  21.8 0.2 constant_dynamic-update-slice_fusion.3
  22.0 1.5 %collective-permute-start.2 = (bf16[128,1024]{1,0:T(8,128)(2,1)S(1)}, bf16[128,1024]{1,0:T(8,128)(2,1)S(1)}, u32[]{:S(2)}, u32[]{:S(2)}) collective-permute-start(bf16[128,1024]{1,0:T(8,128)(2,1)S(1)} %get-tuple-element.3), channel_id=1, source_target_pairs={{0,4},{4,8},{8,12},{12,0},{1,5},{5,9},{9,13},{13,1},{2,6},{6,10},{... | collective-permute-start | bytes 786440 | tf_op jit(solution)/shard_map/ppermute | solution.py:17
  23.6 0.1 compare_reduce_fusion
  23.6 0.1 copy.48
  23.8 1.5 %collective-permute-start.3 = (bf16[128,1024]{1,0:T(8,128)(2,1)S(1)}, bf16[128,1024]{1,0:T(8,128)(2,1)S(1)}, u32[]{:S(2)}, u32[]{:S(2)}) collective-permute-start(bf16[128,1024]{1,0:T(8,128)(2,1)S(1)} %get-tuple-element.3), channel_id=1, source_target_pairs={{0,12},{4,0},{8,4},{12,8},{1,13},{5,1},{9,5},{13,9},{2,14},{6,2},{... | collective-permute-start | bytes 786440 | tf_op jit(solution)/shard_map/ppermute | solution.py:20
  25.3 6.9 %collective-permute-done.2 = bf16[128,1024]{1,0:T(8,128)(2,1)S(1)} collective-permute-done((bf16[128,1024]{1,0:T(8,128)(2,1)S(1)}, bf16[128,1024]{1,0:T(8,128)(2,1)S(1)}, u32[]{:S(2)}, u32[]{:S(2)}) %collective-permute-start.2) | collective-permute-done | bytes 262176 | tf_op jit(solution)/shard_map/ppermute | solution.py:17
  32.1 0.6 collective-permute-start.4
  32.7 0.1 copy.49
  32.8 0.1 copy.50
  32.9 4.9 %collective-permute-done.3 = bf16[128,1024]{1,0:T(8,128)(2,1)S(1)} collective-permute-done((bf16[128,1024]{1,0:T(8,128)(2,1)S(1)}, bf16[128,1024]{1,0:T(8,128)(2,1)S(1)}, u32[]{:S(2)}, u32[]{:S(2)}) %collective-permute-start.3) | collective-permute-done | bytes 262176 | tf_op jit(solution)/shard_map/ppermute | solution.py:20
  37.8 4.7 %collective-permute-done.4 = bf16[128,1024]{1,0:T(8,128)(2,1)S(1)} collective-permute-done((bf16[128,1024]{1,0:T(8,128)(2,1)S(1)}, bf16[128,1024]{1,0:T(8,128)(2,1)S(1)}, u32[]{:S(2)}, u32[]{:S(2)}) %collective-permute-start.4) | collective-permute-done | bytes 262176 | tf_op jit(solution)/shard_map/ppermute | solution.py:17
  42.6 1.2 convolution_convert_fusion.1
  43.9 1.1 copy.52
  44.9 5.7 %all-to-all-start = ((bf16[4,2,8,4096]{3,2,1,0:T(8,128)(2,1)}), bf16[4,2,8,4096]{3,2,1,0:T(8,128)(2,1)S(1)}, u32[]{:S(2)}, u32[]{:S(2)}) async-start(bf16[4,2,8,4096]{3,2,1,0:T(8,128)(2,1)} %copy.52), calls=%async_computation | async-start | bytes 1048576 | tf_op jit(solution)/shard_map/all_to_all | solution.py:90
  50.6 0.7 all-gather.2.cloned.1.call-update
  51.3 0.0 reduce-scatter.2.cloned.1.call-start
  51.4 0.1 reshape.78
  51.5 0.1 reduce_sum.18
  51.6 0.1 fusion.19
  51.7 12.9 %all-to-all-done = bf16[4,2,8,4096]{3,2,1,0:T(8,128)(2,1)S(1)} async-done(((bf16[4,2,8,4096]{3,2,1,0:T(8,128)(2,1)}), bf16[4,2,8,4096]{3,2,1,0:T(8,128)(2,1)S(1)}, u32[]{:S(2)}, u32[]{:S(2)}) %all-to-all-start) | async-done | bytes 524320 | tf_op jit(solution)/shard_map/all_to_all | solution.py:90
  64.6 0.3 fusion.25
  64.9 0.3 convolution_convert_fusion.2
  65.2 0.5 copy.54
  65.7 16.5 %all_to_all.15 = bf16[4,2,8,4096]{3,1,2,0:T(2,128)(2,1)S(1)} all-to-all(bf16[4,2,8,4096]{3,1,2,0:T(2,128)(2,1)S(1)} %copy.54), channel_id=1, replica_groups=mesh['pair'=2,'lat'=4,'tok'=4] {'tok'}, dimensions={0} | all-to-all | bytes 1048576 | tf_op jit(solution)/shard_map/all_to_all | solution.py:108
  82.2 0.7 fusion
  82.9 1.6 %copy.76 = bf16[16,8,4096]{2,1,0:T(8,128)(2,1)} copy(bf16[16,8,4096]{2,0,1:T(8,128)(2,1)S(1)} %fusion) | data formatting | bytes 2097152 | tf_op jit(solution)/shard_map/convert_element_type | solution.py:113
  84.5 0.0 reduce-scatter.2.cloned.1.call-update
  84.5 0.0 all-gather.2.cloned.1.call-done
  84.6 2.5 %convolution_convert_fusion = bf16[4,2,8,4096]{3,0,2,1:T(4,128)(2,1)S(1)} fusion(bf16[16,8,4096]{2,1,0:T(8,128)(2,1)} %bitcast.55, s32[4,16]{1,0:T(4,128)S(1)} %copy.50, s32[4,16]{1,0:T(4,128)S(1)} %copy.49), kind=kOutput, calls=%fused_computation.3 | convolution fusion | flops 8651136 | bytes 1573376 | tf_op jit(solution)/shard_map/ksb,btd->kstd/dot_general | solution.py:78
  87.0 1.1 copy.58
  88.1 3.5 %all-to-all-start.2 = ((bf16[4,2,8,4096]{3,2,1,0:T(8,128)(2,1)}), bf16[4,2,8,4096]{3,2,1,0:T(8,128)(2,1)S(1)}, u32[]{:S(2)}, u32[]{:S(2)}) async-start(bf16[4,2,8,4096]{3,2,1,0:T(8,128)(2,1)} %copy.58), calls=%async_computation.3 | async-start | bytes 1048576 | tf_op jit(solution)/shard_map/all_to_all | solution.py:91
  91.6 0.0 all-reduce.2.cloned.1.call-start
  91.7 19.6 %reduce-scatter.2.cloned.1.call-done = bf16[128,1024]{1,0:T(8,128)(2,1)} async-done(((bf16[128,4096]{1,0:T(8,128)(2,1)}), bf16[128,1024]{1,0:T(8,128)(2,1)}) %reduce-scatter.2.cloned.1.call-update) | async-done | bytes 262160 | tf_op jit(solution)/shard_map/reduce_scatter | solution.py:112
  111.3 0.5 fusion.3
  111.7 0.5 broadcast_multiply_fusion
  112.3 19.5 %all-reduce.2.cloned.1.call-done = bf16[128,1024]{1,0:T(8,128)(2,1)} async-done(((bf16[128,1024]{1,0:T(8,128)(2,1)}), bf16[128,1024]{1,0:T(8,128)(2,1)}) %all-reduce.2.cloned.1.call-update) | async-done | bytes 262160 | tf_op jit(solution)/shard_map/psum | solution.py:115
  131.8 1.7 %add_convert_fusion = bf16[128,1024]{1,0:T(8,128)(2,1)} fusion(bf16[128,1024]{1,0:T(8,128)(2,1)} %all-reduce.2.cloned.1.call-done, f32[1024]{0:T(1024)S(1)} %copy-done.2), kind=kLoop, calls=%fused_computation.21 | loop fusion | flops 393216 | bytes 528384 | tf_op jit(solution)/shard_map/convert_element_type | solution.py:116
  (23 shorter events, 0.2 us)
Async XLA Ops:
  7.2 57.7 %copy-start = (bf16[128,4096]{1,0:T(8,128)(2,1)S(1)}, bf16[128,4096]{1,0:T(8,128)(2,1)}, u32[]{:S(2)}) copy-start(bf16[128,4096]{1,0:T(8,128)(2,1)} %param.14) | copy-start | bytes 3145732
  7.2 11.0 %collective-permute-start = (bf16[128,1024]{1,0:T(8,128)(2,1)}, bf16[128,1024]{1,0:T(8,128)(2,1)S(1)}, u32[]{:S(2)}, u32[]{:S(2)}) collective-permute-start(bf16[128,1024]{1,0:T(8,128)(2,1)} %bitcast.56), channel_id=1, source_target_pairs={{0,1},{1,2},{2,3},{4,5},{5,6},{6,7},{8,9},{9,10},{10,11},{12,13},{... | collective-permute-start | bytes 786440 | tf_op jit(solution)/shard_map/ppermute | solution.py:30
  19.1 1.1 copy-start.3
  20.1 1.6 %collective-permute-start.1 = (bf16[128,1024]{1,0:T(8,128)(2,1)S(1)}, bf16[128,1024]{1,0:T(8,128)(2,1)S(1)}, u32[]{:S(2)}, u32[]{:S(2)}) collective-permute-start(bf16[128,1024]{1,0:T(8,128)(2,1)S(1)} %broadcast_select_fusion), channel_id=1, source_target_pairs={{0,16},{16,0},{1,17},{17,1},{2,18},{18,2},{3,19},{19,3},{4,20},{20... | collective-permute-start | bytes 786440 | tf_op jit(solution)/shard_map/ppermute | solution.py:34
  22.0 10.1 %collective-permute-start.2 = (bf16[128,1024]{1,0:T(8,128)(2,1)S(1)}, bf16[128,1024]{1,0:T(8,128)(2,1)S(1)}, u32[]{:S(2)}, u32[]{:S(2)}) collective-permute-start(bf16[128,1024]{1,0:T(8,128)(2,1)S(1)} %get-tuple-element.3), channel_id=1, source_target_pairs={{0,4},{4,8},{8,12},{12,0},{1,5},{5,9},{9,13},{13,1},{2,6},{6,10},{... | collective-permute-start | bytes 786440 | tf_op jit(solution)/shard_map/ppermute | solution.py:17
  23.8 14.0 %collective-permute-start.3 = (bf16[128,1024]{1,0:T(8,128)(2,1)S(1)}, bf16[128,1024]{1,0:T(8,128)(2,1)S(1)}, u32[]{:S(2)}, u32[]{:S(2)}) collective-permute-start(bf16[128,1024]{1,0:T(8,128)(2,1)S(1)} %get-tuple-element.3), channel_id=1, source_target_pairs={{0,12},{4,0},{8,4},{12,8},{1,13},{5,1},{9,5},{13,9},{2,14},{6,2},{... | collective-permute-start | bytes 786440 | tf_op jit(solution)/shard_map/ppermute | solution.py:20
  32.1 10.4 %collective-permute-start.4 = (bf16[128,1024]{1,0:T(8,128)(2,1)S(1)}, bf16[128,1024]{1,0:T(8,128)(2,1)S(1)}, u32[]{:S(2)}, u32[]{:S(2)}) collective-permute-start(bf16[128,1024]{1,0:T(8,128)(2,1)S(1)} %collective-permute-done.2), channel_id=1, source_target_pairs={{0,4},{4,8},{8,12},{12,0},{1,5},{5,9},{9,13},{13,1},{2,6},{6,10},{... | collective-permute-start | bytes 786440 | tf_op jit(solution)/shard_map/ppermute | solution.py:17
  43.8 20.7 %copy-start.1 = (bf16[4096,128]{1,0:T(8,128)(2,1)S(1)}, bf16[4096,128]{1,0:T(8,128)(2,1)}, u32[]{:S(2)}) copy-start(bf16[4096,128]{1,0:T(8,128)(2,1)} %param.12) | copy-start | bytes 3145732
  43.8 20.7 %copy-start.4 = (f32[128]{0:T(128)S(1)}, f32[128]{0:T(128)}, u32[]{:S(2)}) copy-start(f32[128]{0:T(128)} %param.13) | copy-start | bytes 1540
  44.9 19.6 %all-to-all-start = ((bf16[4,2,8,4096]{3,2,1,0:T(8,128)(2,1)}), bf16[4,2,8,4096]{3,2,1,0:T(8,128)(2,1)S(1)}, u32[]{:S(2)}, u32[]{:S(2)}) async-start(bf16[4,2,8,4096]{3,2,1,0:T(8,128)(2,1)} %copy.52), calls=%async_computation | async-start | bytes 1048576 | tf_op jit(solution)/shard_map/all_to_all | solution.py:90
  50.6 33.9 %all-gather.2.cloned.1.call-start = ((), (), s32[]{:S(2)}) async-start(), calls=%async_computation.6 | async-start | bytes 1310720 | tf_op jit(solution)/shard_map/all_gather | solution.py:84
  51.3 59.9 %reduce-scatter.2.cloned.1.call-start = ((), (), s32[]{:S(2)}) async-start(), calls=%async_computation.4 | async-start | bytes 1310720 | tf_op jit(solution)/shard_map/reduce_scatter | solution.py:112
  88.1 23.1 %all-to-all-start.2 = ((bf16[4,2,8,4096]{3,2,1,0:T(8,128)(2,1)}), bf16[4,2,8,4096]{3,2,1,0:T(8,128)(2,1)S(1)}, u32[]{:S(2)}, u32[]{:S(2)}) async-start(bf16[4,2,8,4096]{3,2,1,0:T(8,128)(2,1)} %copy.58), calls=%async_computation.3 | async-start | bytes 1048576 | tf_op jit(solution)/shard_map/all_to_all | solution.py:91
  91.6 40.2 %copy-start.2 = (f32[1024]{0:T(1024)S(1)}, f32[1024]{0:T(1024)}, u32[]{:S(2)}) copy-start(f32[1024]{0:T(1024)} %param.15) | copy-start | bytes 12292
  91.6 40.2 %all-reduce.2.cloned.1.call-start = ((), (), s32[]{:S(2)}) async-start(), calls=%async_computation.5 | async-start | bytes 524288 | tf_op jit(solution)/shard_map/psum | solution.py:115
Sparse Core Ops, SparseCore 0:
  53.3 27.0 all-gather.1
  84.7 26.5 reduce-scatter.1
  113.5 18.2 all-reduce.1
